TPU v7x, 128 devices: a whole 4x4x4 slice. The times are simulated.
128 devices in a mesh: ctx: 16 (over y, z_hi, core), head: 8 (over x, z_lo).
Axes of the slice: x: 4, y: 4, z: 4 (z_hi: 2, z_lo: 2; z = z_hi * 2 + z_lo), core: 2. Of those that a mesh axis runs over, the one named last changes fastest.
Arguments:
- queries: bfloat16 [2048, 12288], P('ctx', 'head'), may hold values from -8 to 8
- latents: bfloat16 [2048, 512], P('ctx'), may hold values from -4 to 4
- rope_key: bfloat16 [2048, 64], P('ctx'), may hold values from -8 to 8
- up_key_weight: bfloat16 [512, 8192], P(None, 'head'), may hold values from -0.5 to 0.5
- up_value_weight: bfloat16 [512, 8192], P(None, 'head'), may hold values from -0.25 to 0.25
- out_grad: bfloat16 [2048, 8192], P('ctx', 'head'), may hold values from -6 to 6
- group_order: int32 [32], replicated, may hold values from 0 to 31, as said below
Outputs:
- query_grad: bfloat16 [2048, 12288], P('ctx', 'head')
- latent_grad: float32 [2048, 512], P('ctx')
- rope_grad: float32 [2048, 64], P('ctx')
- up_key_grad: float32 [512, 8192], P('ctx', 'head')
- up_value_grad: float32 [512, 8192], P('ctx', 'head')
Inputs may be any that keep to these rules, and one draw needn't show every extreme that they name: A permutation of the 32 group numbers; storage slot k (rows k * 64 to k * 64 + 63) holds the sequence positions group_order[k] * 64 on, in order.
All inputs are finite; a program needn't handle non-finite values.
Results may differ from a plain program's by a relative error of at most 0.017.
Values may be sent and summed in bfloat16 or wider, within the bound.
No kernel may reach another device: no remote copies, remote signals or barrier semaphores. Data moves between devices by JAX's collectives and lax.ppermute only.
A program may use at most 64 MiB of HBM per device.

v0:
```python
import jax
import jax.numpy as jnp
from jax import lax
from jax.sharding import PartitionSpec as P

D_LATENT = 512
ROPE = 64
NOPE = 128
VDIM = 128
NEG_FILL = -1e30


def product(pattern, left_side, right_side):
    return jnp.einsum(pattern, left_side, right_side, preferred_element_type=jnp.float32)


def token_positions(group_order, row_ids, group_len):
    slot_ids = row_ids // group_len
    slot_table = jnp.arange(group_order.shape[0], dtype=jnp.int32)
    picked = jnp.sum(
        jnp.where(slot_ids[:, None] == slot_table[None, :], group_order[None, :], 0), axis=1
    )
    return picked * group_len + row_ids % group_len


def per_device(queries, latents, rope_key, up_key_weight, up_value_weight, out_grad, group_order):
    tok_count = queries.shape[0]
    head_count = up_key_weight.shape[1] // NOPE
    group_len = tok_count // 2
    scale_factor = (NOPE + ROPE) ** (-0.5)
    shaped = queries.reshape(tok_count, head_count, NOPE + ROPE)
    query_nope = shaped[:, :, :NOPE]
    query_rope = shaped[:, :, NOPE:]
    up_key = up_key_weight.reshape(D_LATENT, head_count, NOPE)
    up_value = up_value_weight.reshape(D_LATENT, head_count, VDIM)
    grad_out = out_grad.reshape(tok_count, head_count, VDIM)
    query_abs = product("thd,khd->thk", query_nope, up_key).astype(jnp.bfloat16)
    grad_lat = product("thd,khd->thk", grad_out, up_value).astype(jnp.bfloat16)
    own_rows = lax.axis_index("ctx") * tok_count + jnp.arange(tok_count, dtype=jnp.int32)
    query_pos = token_positions(group_order, own_rows, group_len)

    def piece_scores(latent_piece, rope_piece):
        scores = product("thk,nk->thn", query_abs, latent_piece) + product(
            "thr,nr->thn", query_rope, rope_piece
        )
        return scores * scale_factor

    latent_piece = lax.all_gather(latents, "ctx", axis=0, tiled=True)
    rope_piece = lax.all_gather(rope_key, "ctx", axis=0, tiled=True)
    row_count = latent_piece.shape[0]
    key_pos = token_positions(group_order, jnp.arange(row_count, dtype=jnp.int32), group_len)
    visible = key_pos[None, None, :] <= query_pos[:, None, None]
    run_max = jnp.full((tok_count, head_count), NEG_FILL, jnp.float32)
    scores = piece_scores(latent_piece, rope_piece)
    grad_prob = product("thk,nk->thn", grad_lat, latent_piece)
    new_max = jnp.maximum(run_max, jnp.max(jnp.where(visible, scores, NEG_FILL), axis=2))
    weights = jnp.where(visible, jnp.exp(scores - new_max[:, :, None]), 0.0)
    forward_state = (new_max, jnp.sum(weights, axis=2), jnp.sum(weights * grad_prob, axis=2))
    run_max, run_sum, run_dot = forward_state
    log_total = run_max + jnp.log(run_sum)
    row_delta = run_dot / run_sum
    latent_piece = lax.all_gather(latents, "ctx", axis=0, tiled=True)
    rope_piece = lax.all_gather(rope_key, "ctx", axis=0, tiled=True)
    row_count = latent_piece.shape[0]
    key_pos = token_positions(group_order, jnp.arange(row_count, dtype=jnp.int32), group_len)
    visible = key_pos[None, None, :] <= query_pos[:, None, None]
    scores = piece_scores(latent_piece, rope_piece)
    softmax_rows = jnp.where(visible, jnp.exp(scores - log_total[:, :, None]), 0.0)
    grad_prob = product("thk,nk->thn", grad_lat, latent_piece)
    grad_score = softmax_rows * (grad_prob - row_delta[:, :, None]) * scale_factor
    probs_low = softmax_rows.astype(jnp.bfloat16)
    grad_low = grad_score.astype(jnp.bfloat16)
    acc_out = product("thn,nk->thk", probs_low, latent_piece)
    acc_query = product("thn,nk->thk", grad_low, latent_piece)
    acc_rope = product("thn,nr->thr", grad_low, rope_piece)
    latent_part = product("thn,thk->nk", grad_low, query_abs) + product(
        "thn,thk->nk", probs_low, grad_lat
    )
    rope_part = product("thn,thr->nr", grad_low, query_rope)
    all_latent = latent_part
    all_rope = rope_part
    backward_state = (acc_query, acc_rope, acc_out, all_latent, all_rope)
    acc_query, acc_rope, acc_out, all_latent, all_rope = backward_state
    grad_abs = acc_query.astype(jnp.bfloat16)
    grad_nope = product("thk,khd->thd", grad_abs, up_key)
    query_grad = (
        jnp.concatenate([grad_nope, acc_rope], axis=2).astype(jnp.bfloat16).reshape(tok_count, -1)
    )
    out_low = acc_out.astype(jnp.bfloat16)
    weight_key_grad = product("thk,thd->khd", grad_abs, query_nope).reshape(D_LATENT, -1)
    weight_value_grad = product("thk,thd->khd", out_low, grad_out).reshape(D_LATENT, -1)
    up_key_grad, up_value_grad = (
        lax.psum_scatter(
            weight_key_grad.astype(jnp.bfloat16), "ctx", scatter_dimension=0, tiled=True
        ).astype(jnp.float32),
        lax.psum_scatter(
            weight_value_grad.astype(jnp.bfloat16), "ctx", scatter_dimension=0, tiled=True
        ).astype(jnp.float32),
    )
    partial_latent, partial_rope = (
        lax.psum_scatter(
            all_latent.astype(jnp.bfloat16), "ctx", scatter_dimension=0, tiled=True
        ).astype(jnp.float32),
        lax.psum_scatter(
            all_rope.astype(jnp.bfloat16), "ctx", scatter_dimension=0, tiled=True
        ).astype(jnp.float32),
    )
    latent_grad, rope_grad = (
        lax.psum(partial_latent.astype(jnp.bfloat16), "head").astype(jnp.float32),
        lax.psum(partial_rope.astype(jnp.bfloat16), "head").astype(jnp.float32),
    )
    return (query_grad, latent_grad, rope_grad, up_key_grad, up_value_grad)


def solution(mesh):
    placed = (
        P("ctx", "head"),
        P("ctx", None),
        P("ctx", None),
        P(None, "head"),
        P(None, "head"),
        P("ctx", "head"),
        P(),
    )
    return jax.shard_map(
        per_device,
        mesh=mesh,
        in_specs=placed,
        out_specs=(
            P("ctx", "head"),
            P("ctx", None),
            P("ctx", None),
            P("ctx", "head"),
            P("ctx", "head"),
        ),
        check_vma=False,
    )
```

profile of v0, /device:TPU:0, one launch (start us, length us, event | category | flops | bytes accessed | tf_op | source)
XLA Modules:
  0.0 446.0 jit_solution(16935749232204141822)
XLA Ops:
  13.4 26.6 %all_gather.9 = bf16[2048,64]{0,1:T(8,128)(2,1)S(1)} all-gather(bf16[128,64]{0,1:T(8,128)(2,1)} %param.9), channel_id=1, replica_groups=mesh['ctx'=16,'head'=8] {'ctx'}, dimensions={0}, use_global_device_ids=true | all-gather | bytes 278528 | tf_op jit(solution)/shard_map/all_gather | solution.py:63
  43.2 18.1 %all-gather.2.cloned.1.call-done = bf16[2048,512]{1,0:T(8,128)(2,1)} async-done(((bf16[128,512]{1,0:T(8,128)(2,1)}), bf16[2048,512]{1,0:T(8,128)(2,1)}) %all-gather.2.cloned.1.call-update) | async-done | bytes 2097168 | tf_op jit(solution)/shard_map/all_gather | solution.py:62
  61.3 4.3 fusion.10
  65.6 2.2 select_reduce_fusion
  67.9 4.3 fusion
  72.2 3.2 multiply_convert_fusion
  75.5 2.0 copy-done.1
  77.4 2.4 fusion.46
  79.9 4.7 %fusion.2 = bf16[2048,512]{1,0:T(8,128)(2,1)} fusion(f32[2048,512,1]{1,0,2:T(8,128)S(1)} %fusion.46, bf16[128,8,512]{0,2,1:T(8,128)(2,1)S(1)} %copy-done.6, f32[128,8,2048]{2,0,1:T(8,128)S(1)} %get-tuple-element.30, f32[128,8]{0,1:T(8,128)S(1)} %get-tuple-element.27, pred[128,2048]{1,0:T(8,128)(4,1)S(1)} %broadcast_compare_fusion), kind=kOutput, calls=%fused_computation.9 | convolution fusion | flops 2155872256 | bytes 15994880 | tf_op jit(solution)/shard_map/thn,thk->nk/dot_general | solution.py:14
  84.6 3.0 fusion.3
  88.8 7.7 %convolution_convert_fusion.1 = bf16[8,512,128]{1,2,0:T(8,128)(2,1)} fusion(bf16[128,8,128]{0,2,1:T(8,128)(2,1)S(1)} %bitcast.81, bf16[2048,512]{1,0:T(8,128)(2,1)} %all-gather.2.cloned.1.call-done, f32[128,8,2048]{2,0,1:T(8,128)} %copy-done.2, f32[128,8]{0,1:T(8,128)S(1)} %get-tuple-element.27, pred[128,2048]{1,0:T(8,128)(4,1)S(1)} %broadcast_compare_fusion), kind=kOutput, calls=%fused_computation.21 | convolution fusion | flops 2289041408 | bytes 12062720 | tf_op jit(solution)/shard_map/thk,thd->khd/dot_general | solution.py:14
  96.5 2.3 copy.78
  99.1 5.4 %fusion.12 = bf16[128,8,512]{2,0,1:T(8,128)(2,1)S(1)} fusion(bf16[128,8,2048]{2,0,1:T(8,128)(2,1)} %copy-done.1, bf16[2048,512]{1,0:T(8,128)(2,1)} %all-gather.2.cloned.1.call-done), kind=kOutput, calls=%fused_computation.24 | convolution fusion | flops 2148007936 | bytes 7340032 | tf_op jit(solution)/shard_map/thn,nk->thk/dot_general | solution.py:14
  105.9 2.4 copy.76
  109.4 3.6 convolution_convert_fusion.5
  113.1 41.4 %reduce-scatter.7.cloned.1.call-done = bf16[128,512]{1,0:T(8,128)(2,1)} async-done(((bf16[2048,512]{1,0:T(8,128)(2,1)}), bf16[128,512]{1,0:T(8,128)(2,1)}) %reduce-scatter.7.cloned.1.call-update) | async-done | bytes 131088 | tf_op jit(solution)/shard_map/reduce_scatter | solution.py:101
  155.5 67.5 %reduce-scatter.13.cloned.1.call-done = bf16[128,64]{1,0:T(8,128)(2,1)} async-done(((bf16[2048,64]{1,0:T(8,128)(2,1)}), bf16[128,64]{1,0:T(8,128)(2,1)}) %reduce-scatter.13.cloned.1.call-update) | async-done | bytes 16400
  223.8 33.4 %psum.15 = bf16[128,64]{0,1:T(8,128)(2,1)S(1)} all-reduce(bf16[128,64]{0,1:T(8,128)(2,1)S(1)} %copy.88), channel_id=1, replica_groups=mesh['ctx'=16,'head'=8] {'head'}, use_global_device_ids=true, to_apply=%region_8.9 | all-reduce | flops 8192 | bytes 32768 | tf_op jit(solution)/shard_map/psum | solution.py:110
  257.9 34.8 %reduce-scatter.11.cloned.1.call-done = bf16[32,1024]{1,0:T(8,128)(2,1)} async-done(((bf16[512,1024]{1,0:T(8,128)(2,1)}), bf16[32,1024]{1,0:T(8,128)(2,1)}) %reduce-scatter.11.cloned.1.call-update) | async-done | bytes 65552 | tf_op jit(solution)/shard_map/reduce_scatter | solution.py:96
  292.7 1.5 convert_element_type.89
  294.2 68.2 %reduce-scatter.9.cloned.1.call-done = bf16[32,1024]{1,0:T(8,128)(2,1)} async-done(((bf16[512,1024]{1,0:T(8,128)(2,1)}), bf16[32,1024]{1,0:T(8,128)(2,1)}) %reduce-scatter.9.cloned.1.call-update) | async-done | bytes 65552 | tf_op jit(solution)/shard_map/reduce_scatter | solution.py:93
  362.4 1.5 convert_element_type.84
  363.9 73.6 %all-reduce.2.cloned.1.call-done = bf16[128,512]{1,0:T(8,128)(2,1)} async-done(((bf16[128,512]{1,0:T(8,128)(2,1)}), bf16[128,512]{1,0:T(8,128)(2,1)}) %all-reduce.2.cloned.1.call-update) | async-done | bytes 131088 | tf_op jit(solution)/shard_map/psum | solution.py:109
  437.5 1.6 convert_element_type.78
  (50 shorter events, 15.8 us)
Async XLA Ops:
  7.2 34.3 %copy-start = (bf16[512,1024]{1,0:T(8,128)(2,1)S(1)}, bf16[512,1024]{1,0:T(8,128)(2,1)}, u32[]{:S(2)}) copy-start(bf16[512,1024]{1,0:T(8,128)(2,1)} %param.11) | copy-start | bytes 3145732
  7.2 54.1 %all-gather.2.cloned.1.call-start = ((), (), s32[]{:S(2)}) async-start(), calls=%async_computation.4 | async-start | bytes 2228224 | tf_op jit(solution)/shard_map/all_gather | solution.py:62
  7.9 146.6 %reduce-scatter.7.cloned.1.call-start = ((), (), s32[]{:S(2)}) async-start(), calls=%async_computation.5 | async-start | bytes 2228224 | tf_op jit(solution)/shard_map/reduce_scatter | solution.py:101
  39.9 25.7 %copy-start.3 = (bf16[2048,64]{0,1:T(8,128)(2,1)}, bf16[2048,64]{0,1:T(8,128)(2,1)S(1)}, u32[]{:S(2)}) copy-start(bf16[2048,64]{0,1:T(8,128)(2,1)S(1)} %all_gather.9) | copy-start | bytes 786436
  65.6 2.2 copy-start.6
  65.6 2.2 copy-start.8
  67.8 12.0 %copy-start.2 = (f32[128,8,2048]{2,0,1:T(8,128)}, f32[128,8,2048]{2,0,1:T(8,128)S(1)}, u32[]{:S(2)}) copy-start(f32[128,8,2048]{2,0,1:T(8,128)S(1)} %get-tuple-element.30) | copy-start | bytes 25165828
  72.2 5.2 %copy-start.7 = (bf16[128,8,512]{0,2,1:T(8,128)(2,1)S(1)}, bf16[128,8,512]{0,2,1:T(8,128)(2,1)}, u32[]{:S(2)}) copy-start(bf16[128,8,512]{0,2,1:T(8,128)(2,1)} %fusion.18) | copy-start | bytes 3145732
  75.5 2.0 copy-start.1
  84.6 138.4 %reduce-scatter.13.cloned.1.call-start = ((), (), s32[]{:S(2)}) async-start(), calls=%async_computation.9 | async-start | bytes 557056
  88.7 204.0 %reduce-scatter.11.cloned.1.call-start = ((), (), s32[]{:S(2)}) async-start(), calls=%async_computation.8 | async-start | bytes 1114112 | tf_op jit(solution)/shard_map/reduce_scatter | solution.py:96
  98.8 263.6 %reduce-scatter.9.cloned.1.call-start = ((), (), s32[]{:S(2)}) async-start(), calls=%async_computation.7 | async-start | bytes 1114112 | tf_op jit(solution)/shard_map/reduce_scatter | solution.py:93
  105.9 3.6 copy-start.4
  108.2 329.3 %all-reduce.2.cloned.1.call-start = ((), (), s32[]{:S(2)}) async-start(), calls=%async_computation.6 | async-start | bytes 262144 | tf_op jit(solution)/shard_map/psum | solution.py:109
  109.4 45.1 %copy-start.5 = (bf16[128,8,128]{0,2,1:T(8,128)(2,1)S(1)}, bf16[128,8,128]{0,2,1:T(8,128)(2,1)}, u32[]{:S(2)}) copy-start(bf16[128,8,128]{0,2,1:T(8,128)(2,1)} %fusion.22) | copy-start | bytes 786436
Sparse Core Ops, SparseCore 0:
  10.4 50.8 all-gather.1
  84.7 69.7 reduce-scatter.6
  158.3 64.6 reduce-scatter.12
  226.7 65.9 reduce-scatter.10
  296.4 65.9 reduce-scatter.8
  364.7 72.7 all-reduce.1
where the time goes:
time: 447 us; the launch traced here: 446 us
  waiting for transfers between devices  305 us (68%)
  blocking collectives  60 us (13%)
  matrix products  43.2 us (10%)
  between operations  14.3 us (3%)
  local copies, waits for them, and re-layouts  13.3 us (3%)
  other arithmetic  10.3 us (2%)
    psum x1, waiting for transfers between devices, per_device(): lax.psum(partial_latent.astype(jnp.bfloat16), 'head').astype(jnp.float32)  73.6 us
    unnamed x7, waiting for transfers between devices  68.2 us
    reduce_scatter x1, waiting for transfers between devices, per_device(): lax.psum_scatter(weight_key_grad.astype(jnp.bfloat16), 'ctx', scatter_dim...  68.2 us
    dot_general x13, matrix products, product(): jnp.einsum(pattern, left_side, right_side, preferred_element_type=jnp.flo...  43.2 us
    reduce_scatter x1, waiting for transfers between devices, per_device(): lax.psum_scatter(all_latent.astype(jnp.bfloat16), 'ctx', scatter_dimensio...  41.4 us
    reduce_scatter x1, waiting for transfers between devices, per_device(): lax.psum_scatter(weight_value_grad.astype(jnp.bfloat16), 'ctx', scatter_d...  34.8 us
    psum x1, blocking collectives, per_device(): lax.psum(partial_rope.astype(jnp.bfloat16), 'head').astype(jnp.float32)  33.4 us
    all_gather x1, blocking collectives, per_device(): rope_piece = lax.all_gather(rope_key, 'ctx', axis=0, tiled=True)  26.6 us
  transfers between devices with their start and end apart: 6, of which 6 were waited for; matrix products, arithmetic and copies ran while one was open for 9% of the time, Pallas kernels for 0%

commit v1 on v0

--- a/solution.py
+++ b/solution.py
@@ -59,8 +59,11 @@
     run_max, run_sum, run_dot = forward_state
     log_total = run_max + jnp.log(run_sum)
     row_delta = run_dot / run_sum
-    latent_piece = lax.all_gather(latents, "ctx", axis=0, tiled=True)
-    rope_piece = lax.all_gather(rope_key, "ctx", axis=0, tiled=True)
+    latent_piece, rope_piece = jnp.split(
+        lax.all_gather(jnp.concatenate([latents, rope_key], axis=1), "ctx", axis=0, tiled=True),
+        [latents.shape[1]],
+        axis=1,
+    )
     row_count = latent_piece.shape[0]
     key_pos = token_positions(group_order, jnp.arange(row_count, dtype=jnp.int32), group_len)
     visible = key_pos[None, None, :] <= query_pos[:, None, None]

time: 447 us -> 492 us (1.10)
  waiting for transfers between devices: 305 us -> 341 us
  matrix products: 43.2 us -> 52.7 us
    all_gather x0 -> x1, waiting for transfers between devices: none -> 38.2 us  [per_device(): lax.all_gather(jnp.concatenate([latents, rope_key], axis=1), 'ctx', axis=...]
    dot_general x13 -> x16, matrix products: 43.2 us -> 52.7 us  [product(): jnp.einsum(pattern, left_side, right_side, preferred_element_type=jnp.flo...]
    unnamed x7 -> x8, waiting for transfers between devices: 68.2 us -> 68.1 us
  transfers between devices with their start and end apart: 6 -> 7, of which waited for: 6 -> 7; matrix products, arithmetic and copies ran while one was open for 9% -> 12% of each run, Pallas kernels for 0% -> 0%
where the time goes in v1:
time: 492 us; the launch traced here: 491 us
  waiting for transfers between devices  341 us (69%)
  blocking collectives  59.8 us (12%)
  matrix products  52.7 us (11%)
  between operations  14.4 us (3%)
  local copies, waits for them, and re-layouts  12.1 us (2%)
  other arithmetic  10.7 us (2%)
    psum x1, waiting for transfers between devices, per_device(): lax.psum(partial_latent.astype(jnp.bfloat16), 'head').astype(jnp.float32)  73.8 us
    reduce_scatter x1, waiting for transfers between devices, per_device(): lax.psum_scatter(weight_key_grad.astype(jnp.bfloat16), 'ctx', scatter_dim...  68.2 us
    unnamed x8, waiting for transfers between devices  68.1 us
    dot_general x16, matrix products, product(): jnp.einsum(pattern, left_side, right_side, preferred_element_type=jnp.flo...  52.7 us
    reduce_scatter x1, waiting for transfers between devices, per_device(): lax.psum_scatter(all_latent.astype(jnp.bfloat16), 'ctx', scatter_dimensio...  42.2 us
    all_gather x1, waiting for transfers between devices, per_device(): lax.all_gather(jnp.concatenate([latents, rope_key], axis=1), 'ctx', axis=...  38.2 us
    reduce_scatter x1, waiting for transfers between devices, per_device(): lax.psum_scatter(weight_value_grad.astype(jnp.bfloat16), 'ctx', scatter_d...  34.8 us
    psum x1, blocking collectives, per_device(): lax.psum(partial_rope.astype(jnp.bfloat16), 'head').astype(jnp.float32)  33.4 us
  transfers between devices with their start and end apart: 7, of which 7 were waited for; matrix products, arithmetic and copies ran while one was open for 12% of the time, Pallas kernels for 0%

profile of v1, /device:TPU:0, one launch (start us, length us, event | category | flops | bytes accessed | tf_op | source)
XLA Modules:
  0.0 491.2 jit_solution(16925139374184329437)
XLA Ops:
  10.5 26.4 %all_gather.11 = bf16[2048,64]{0,1:T(8,128)(2,1)S(1)} all-gather(bf16[128,64]{0,1:T(8,128)(2,1)} %param.9), channel_id=1, replica_groups=mesh['ctx'=16,'head'=8] {'ctx'}, dimensions={0}, use_global_device_ids=true | all-gather | bytes 278528 | tf_op jit(solution)/shard_map/all_gather | solution.py:49
  45.5 15.9 %all-gather.5.cloned.1.call-done = bf16[2048,512]{1,0:T(8,128)(2,1)} async-done(((bf16[128,512]{1,0:T(8,128)(2,1)}), bf16[2048,512]{1,0:T(8,128)(2,1)}) %all-gather.5.cloned.1.call-update) | async-done | bytes 2097168 | tf_op jit(solution)/shard_map/all_gather | solution.py:48
  61.3 4.3 fusion.8
  65.7 2.2 select_reduce_fusion
  67.9 2.0 fusion.4
  69.9 5.0 %multiply_reduce_fusion = f32[128,8]{0,1:T(8,128)S(1)} fusion(f32[128,8,2048]{2,0,1:T(8,128)S(1)} %get-tuple-element.28, bf16[128,8,512]{0,2,1:T(8,128)(2,1)S(1)} %copy-done.3, f32[128,8]{0,1:T(8,128)S(1)} %broadcast_maximum_fusion, pred[128,2048]{1,0:T(8,128)(4,1)S(1)} %broadcast_compare_fusion, bf16[2048,512]{1,0:T(8,128)(2,1)S(1)} %copy-done.7), kind=kOutput, calls=%fused_computation.6 | convolution fusion | flops 2155871232 | bytes 11804672 | tf_op jit(solution)/shard_map/thk,nk->thn/dot_general | solution.py:14
  74.9 38.2 %all-gather.3.cloned.1.call-done = bf16[2048,576]{1,0:T(8,128)(2,1)} async-done(((bf16[128,576]{1,0:T(8,128)(2,1)}), bf16[2048,576]{1,0:T(8,128)(2,1)}) %all-gather.3.cloned.1.call-update) | async-done | bytes 2359312 | tf_op jit(solution)/shard_map/all_gather | solution.py:63
  113.2 4.4 fusion.23
  117.6 2.6 fusion.3
  120.3 3.2 multiply_convert_fusion
  123.5 2.4 fusion.40
  126.0 4.0 fusion.5
  130.0 3.0 fusion.6
  134.1 7.7 %convolution_convert_fusion.1 = bf16[8,512,128]{1,2,0:T(8,128)(2,1)} fusion(bf16[128,8,128]{0,2,1:T(8,128)(2,1)S(1)} %bitcast.92, f32[128,8,2048]{2,0,1:T(8,128)} %copy-done.2, bf16[2048,576]{1,0:T(8,128)(2,1)} %all-gather.3.cloned.1.call-done), kind=kOutput, calls=%fused_computation.23 | convolution fusion | flops 2284847104 | bytes 11796480 | tf_op jit(solution)/shard_map/thk,thd->khd/dot_general | solution.py:14
  141.8 2.3 copy.103
  144.2 5.4 %convolution_convert_fusion.4 = bf16[128,8,512]{2,0,1:T(8,128)(2,1)S(1)} fusion(bf16[128,8,2048]{2,0,1:T(8,128)(2,1)} %copy-done.1, bf16[2048,576]{1,0:T(8,128)(2,1)} %all-gather.3.cloned.1.call-done), kind=kOutput, calls=%fused_computation.27 | convolution fusion | flops 2148007936 | bytes 7340032 | tf_op jit(solution)/shard_map/thn,nk->thk/dot_general | solution.py:14
  151.0 2.3 copy.101
  153.8 3.7 convolution_convert_fusion.6
  157.5 42.2 %reduce-scatter.7.cloned.1.call-done = bf16[128,512]{1,0:T(8,128)(2,1)} async-done(((bf16[2048,512]{1,0:T(8,128)(2,1)}), bf16[128,512]{1,0:T(8,128)(2,1)}) %reduce-scatter.7.cloned.1.call-update) | async-done | bytes 131088 | tf_op jit(solution)/shard_map/reduce_scatter | solution.py:104
  200.7 67.3 %reduce-scatter.13.cloned.1.call-done = bf16[128,64]{1,0:T(8,128)(2,1)} async-done(((bf16[2048,64]{1,0:T(8,128)(2,1)}), bf16[128,64]{1,0:T(8,128)(2,1)}) %reduce-scatter.13.cloned.1.call-update) | async-done | bytes 16400
  268.9 33.4 %psum.15 = bf16[128,64]{0,1:T(8,128)(2,1)S(1)} all-reduce(bf16[128,64]{0,1:T(8,128)(2,1)S(1)} %copy.120), channel_id=1, replica_groups=mesh['ctx'=16,'head'=8] {'head'}, use_global_device_ids=true, to_apply=%region_8.9 | all-reduce | flops 8192 | bytes 32768 | tf_op jit(solution)/shard_map/psum | solution.py:113
  302.9 34.8 %reduce-scatter.11.cloned.1.call-done = bf16[32,1024]{1,0:T(8,128)(2,1)} async-done(((bf16[512,1024]{1,0:T(8,128)(2,1)}), bf16[32,1024]{1,0:T(8,128)(2,1)}) %reduce-scatter.11.cloned.1.call-update) | async-done | bytes 65552 | tf_op jit(solution)/shard_map/reduce_scatter | solution.py:99
  339.2 68.2 %reduce-scatter.9.cloned.1.call-done = bf16[32,1024]{1,0:T(8,128)(2,1)} async-done(((bf16[512,1024]{1,0:T(8,128)(2,1)}), bf16[32,1024]{1,0:T(8,128)(2,1)}) %reduce-scatter.9.cloned.1.call-update) | async-done | bytes 65552 | tf_op jit(solution)/shard_map/reduce_scatter | solution.py:96
  408.9 73.8 %all-reduce.2.cloned.1.call-done = bf16[128,512]{1,0:T(8,128)(2,1)} async-done(((bf16[128,512]{1,0:T(8,128)(2,1)}), bf16[128,512]{1,0:T(8,128)(2,1)}) %all-reduce.2.cloned.1.call-update) | async-done | bytes 131088 | tf_op jit(solution)/shard_map/psum | solution.py:112
  (56 shorter events, 22.0 us)
Async XLA Ops:
  7.2 35.1 %copy-start = (bf16[512,1024]{1,0:T(8,128)(2,1)S(1)}, bf16[512,1024]{1,0:T(8,128)(2,1)}, u32[]{:S(2)}) copy-start(bf16[512,1024]{1,0:T(8,128)(2,1)} %param.11) | copy-start | bytes 3145732
  7.2 54.2 %all-gather.5.cloned.1.call-start = ((), (), s32[]{:S(2)}) async-start(), calls=%async_computation.5 | async-start | bytes 2228224 | tf_op jit(solution)/shard_map/all_gather | solution.py:48
  7.9 105.3 %all-gather.3.cloned.1.call-start = ((), (), s32[]{:S(2)}) async-start(), calls=%async_computation.4 | async-start | bytes 2785280 | tf_op jit(solution)/shard_map/all_gather | solution.py:63
  10.4 189.3 %reduce-scatter.7.cloned.1.call-start = ((), (), s32[]{:S(2)}) async-start(), calls=%async_computation.6 | async-start | bytes 2228224 | tf_op jit(solution)/shard_map/reduce_scatter | solution.py:104
  67.9 2.0 copy-start.3
  67.9 2.0 copy-start.7
  113.2 4.5 copy-start.6
  117.6 2.6 copy-start.4
  120.2 5.7 %copy-start.2 = (f32[128,8,2048]{2,0,1:T(8,128)}, f32[128,8,2048]{2,0,1:T(8,128)S(1)}, u32[]{:S(2)}) copy-start(f32[128,8,2048]{2,0,1:T(8,128)S(1)} %fusion.3) | copy-start | bytes 25165828
  120.2 3.3 copy-start.5
  123.5 2.4 copy-start.1
  130.0 138.1 %reduce-scatter.13.cloned.1.call-start = ((), (), s32[]{:S(2)}) async-start(), calls=%async_computation.10 | async-start | bytes 557056
  134.1 203.6 %reduce-scatter.11.cloned.1.call-start = ((), (), s32[]{:S(2)}) async-start(), calls=%async_computation.9 | async-start | bytes 1114112 | tf_op jit(solution)/shard_map/reduce_scatter | solution.py:99
  144.2 263.2 %reduce-scatter.9.cloned.1.call-start = ((), (), s32[]{:S(2)}) async-start(), calls=%async_computation.8 | async-start | bytes 1114112 | tf_op jit(solution)/shard_map/reduce_scatter | solution.py:96
  153.3 329.4 %all-reduce.2.cloned.1.call-start = ((), (), s32[]{:S(2)}) async-start(), calls=%async_computation.7 | async-start | bytes 262144 | tf_op jit(solution)/shard_map/psum | solution.py:112
Sparse Core Ops, SparseCore 0:
  10.4 50.9 all-gather.4
  64.3 48.8 all-gather.2
  130.1 69.6 reduce-scatter.6
  203.3 64.6 reduce-scatter.12
  271.7 65.9 reduce-scatter.10
  341.4 65.9 reduce-scatter.8
  409.9 72.8 all-reduce.1
